TPU v7x, 512 devices: a whole 4x8x8 slice. The times are simulated.
512 devices in a mesh: req: 128 (over z_lo, y, x), tp: 4 (over z_hi, core).
Axes of the slice: x: 4, y: 8, z: 8 (z_hi: 2, z_lo: 4; z = z_hi * 4 + z_lo), core: 2. Of those that a mesh axis runs over, the one named last changes fastest.
Arguments:
- tokens: bfloat16 [8192, 2048], P('req', 'tp'), may hold values from -6 to 6
- expert_in: bfloat16 [128, 2, 2048, 1408], P('req', None, None, 'tp'), may hold values from -0.125 to 0.125
- expert_down: bfloat16 [128, 1408, 2048], P('req', 'tp'), may hold values from -0.15625 to 0.15625
- routes: int32 [8192, 6], P('req'), may hold values from 0 to 127, all different within a row; in each aligned block of 64 rows (0 to 63, 64 to 127, ...) at most 4 rows name the same one
- route_weight: float32 [8192, 6], P('req'), may hold values from 0.1 to 1
Outputs:
- mixed_out: bfloat16 [8192, 2048], P('req', 'tp')
Inputs may be any that keep to these rules, and one draw needn't show every extreme that they name: `routes`: each row names 6 different experts. In each aligned block of 64 rows (the rows of one index of req) no expert is named by more than 4 rows, a bound that some block reaches; every expert is named somewhere.
All inputs are finite; a program needn't handle non-finite values.
Results may differ from a plain program's by a relative error of at most 0.012.
Values may be sent and summed in bfloat16 or wider, within the bound.
A program may use at most 64 MiB of HBM per device.

v0:
```python
import jax
import jax.numpy as jnp
from jax import lax
from jax.sharding import PartitionSpec as P


def per_device(tokens, expert_in, expert_down, routes, route_weight):
    tok_rows = tokens.shape[0]
    top_count = routes.shape[1]
    experts_all = lax.axis_size("req") * expert_in.shape[0]
    capacity = min(tok_rows, max(2, 4 * tok_rows * top_count // (3 * experts_all)))
    buffer_rows = experts_all * capacity
    flat_routes = routes.reshape(-1)
    onehot = (flat_routes[:, None] == jnp.arange(experts_all, dtype=jnp.int32)[None, :]).astype(
        jnp.int32
    )
    earlier = jnp.cumsum(onehot, axis=0) - onehot
    slot_index = jnp.sum(earlier * onehot, axis=1)
    position = (flat_routes * capacity + slot_index).reshape(tok_rows, top_count)
    chooser = jnp.any(
        position[None, :, :] == jnp.arange(buffer_rows, dtype=jnp.int32)[:, None, None], axis=2
    ).astype(jnp.bfloat16)
    whole_rows = lax.all_gather(tokens, "tp", axis=1, tiled=True)
    outgoing = jnp.dot(chooser, whole_rows, preferred_element_type=jnp.float32).astype(jnp.bfloat16)
    outgoing = outgoing.reshape(experts_all, capacity, -1)
    received = lax.all_to_all(outgoing, "req", split_axis=0, concat_axis=0, tiled=True)
    sources, item_count, feature_width = received.shape
    row_block = received.reshape(sources * item_count, feature_width)
    gate_sums = jnp.dot(row_block, expert_in[0, 0], preferred_element_type=jnp.float32)
    up_sums = jnp.dot(row_block, expert_in[0, 1], preferred_element_type=jnp.float32)
    hidden = (jax.nn.silu(gate_sums) * up_sums).astype(jnp.bfloat16)
    partial_value = jnp.dot(hidden, expert_down[0], preferred_element_type=jnp.float32)
    shares = lax.psum_scatter(
        partial_value.astype(jnp.bfloat16), "tp", scatter_dimension=1, tiled=True
    )
    shares = shares.reshape(sources, item_count, -1)
    returned = lax.all_to_all(shares, "req", split_axis=0, concat_axis=0, tiled=True)
    back_flat = returned.reshape(buffer_rows, -1)
    picked = back_flat[position]
    mixed_out = jnp.sum(route_weight[:, :, None] * picked.astype(jnp.float32), axis=1)
    return mixed_out.astype(jnp.bfloat16)


def solution(mesh):
    placed = (
        P("req", "tp"),
        P("req", None, None, "tp"),
        P("req", "tp", None),
        P("req", None),
        P("req", None),
    )
    return jax.shard_map(
        per_device, mesh=mesh, in_specs=placed, out_specs=P("req", "tp"), check_vma=False
    )
```

profile of v0, /device:TPU:1, one launch (start us, length us, event | category | flops | bytes accessed | tf_op | source)
XLA Modules:
  0.0 207.2 jit_solution(7521592075828457885)
XLA Ops:
  6.5 0.0 copy-start
  6.5 0.0 reduce-scatter.2.cloned.1.call-start
  6.5 0.9 copy.24
  7.4 0.1 eq.42
  7.6 0.1 eq.38
  7.7 0.1 copy.26
  7.8 0.2 fusion.22
  8.1 0.1 broadcast_add_fusion
  8.2 0.2 fusion.25
  8.4 0.1 reduce_sum.21
  8.5 0.1 copy.28
  8.6 0.7 compare_select_fusion
  9.3 0.2 fusion.15
  9.5 16.6 %all_gather.3 = bf16[64,2048]{1,0:T(8,128)(2,1)S(1)} all-gather(bf16[64,512]{1,0:T(8,128)(2,1)} %param.5), channel_id=1, replica_groups=mesh['req'=128,'tp'=4] {'tp'}, dimensions={1}, use_global_device_ids=true | all-gather | bytes 327680 | tf_op jit(solution)/shard_map/all_gather | solution.py:23
  26.1 0.7 convolution_convert_fusion.1
  26.9 2.2 %reshape.40 = bf16[128,4,2048]{2,1,0:T(4,128)(2,1)} reshape(bf16[512,2048]{1,0:T(8,128)(2,1)S(1)} %convolution_convert_fusion.1) | data formatting | bytes 4194304 | tf_op jit(solution)/shard_map/reshape | solution.py:25
  29.1 62.5 %all_to_all.10 = bf16[128,4,2048]{2,1,0:T(4,128)(2,1)S(1)} all-to-all(bf16[128,4,2048]{2,1,0:T(4,128)(2,1)} %reshape.40), channel_id=1, replica_groups=mesh['req'=128,'tp'=4] {'req'}, dimensions={0} | all-to-all | bytes 4194304 | tf_op jit(solution)/shard_map/all_to_all | solution.py:26
  91.6 2.1 reshape.41
  93.7 0.0 copy-start.1
  93.7 4.0 %fusion.3 = f32[512,352]{0,1:T(8,128)} fusion(bf16[512,2048]{1,0:T(8,128)(2,1)} %reshape.41, bf16[1,2,2048,352]{2,3,1,0:T(8,128)(2,1)} %param.6), kind=kOutput, calls=%fused_computation.6 | convolution fusion | flops 738197504 | bytes 4259840 | tf_op jit(solution)/shard_map/dot_general | solution.py:29
  97.6 0.0 copy-done
  97.6 0.0 copy-done.1
  97.6 5.1 %convolution_convert_fusion = bf16[512,2048]{1,0:T(8,128)(2,1)} fusion(bf16[1,352,2048]{2,1,0:T(8,128)(2,1)S(1)} %copy-done, bf16[512,2048]{1,0:T(8,128)(2,1)S(1)} %copy-done.1, bf16[1,2,2048,352]{2,3,1,0:T(8,128)(2,1)} %param.6, f32[512,352]{0,1:T(8,128)} %fusion.3), kind=kOutput, calls=%fused_computation.1 | convolution fusion | flops 1478524928 | bytes 7798784 | tf_op jit(solution)/shard_map/dot_general | solution.py:32
  102.7 0.0 copy-start.2
  102.7 0.0 reduce-scatter.2.cloned.1.call-update
  102.8 62.8 %reduce-scatter.2.cloned.1.call-done = bf16[512,512]{1,0:T(8,128)(2,1)} async-done(((bf16[512,2048]{1,0:T(8,128)(2,1)}), bf16[512,512]{1,0:T(8,128)(2,1)}) %reduce-scatter.2.cloned.1.call-update) | async-done | bytes 524304 | tf_op jit(solution)/shard_map/reduce_scatter | solution.py:33
  165.6 2.0 reshape.42
  167.5 11.8 %all-to-all-start.1 = ((bf16[128,4,512]{2,1,0:T(4,128)(2,1)}), bf16[128,4,512]{2,1,0:T(4,128)(2,1)S(1)}, u32[]{:S(2)}, u32[]{:S(2)}) async-start(bf16[128,4,512]{2,1,0:T(4,128)(2,1)} %reshape.42), calls=%async_computation.2 | async-start | bytes 1048576 | tf_op jit(solution)/shard_map/all_to_all | solution.py:37
  179.3 0.1 copy.29
  179.4 0.1 reshape.46
  179.6 0.0 copy-done.2
  179.6 0.1 copy.23
  179.7 17.4 %all-to-all-done.1 = bf16[128,4,512]{2,1,0:T(4,128)(2,1)S(1)} async-done(((bf16[128,4,512]{2,1,0:T(4,128)(2,1)}), bf16[128,4,512]{2,1,0:T(4,128)(2,1)S(1)}, u32[]{:S(2)}, u32[]{:S(2)}) %all-to-all-start.1) | async-done | bytes 524320 | tf_op jit(solution)/shard_map/all_to_all | solution.py:37
  197.0 0.1 reshape.43
  197.2 2.1 gather_fusion
  199.2 0.1 reshape.54
  199.3 1.0 multiply_reduce_fusion
  (4 shorter events, 0.1 us)
Async XLA Ops:
  6.5 91.1 %copy-start = (bf16[1,352,2048]{2,1,0:T(8,128)(2,1)S(1)}, bf16[1,352,2048]{2,1,0:T(8,128)(2,1)}, u32[]{:S(2)}) copy-start(bf16[1,352,2048]{2,1,0:T(8,128)(2,1)} %param.7) | copy-start | bytes 4325380
  6.5 159.0 %reduce-scatter.2.cloned.1.call-start = ((), (), s32[]{:S(2)}) async-start(), calls=%async_computation.3 | async-start | bytes 2621440 | tf_op jit(solution)/shard_map/reduce_scatter | solution.py:33
  93.7 4.0 %copy-start.1 = (bf16[512,2048]{1,0:T(8,128)(2,1)S(1)}, bf16[512,2048]{1,0:T(8,128)(2,1)}, u32[]{:S(2)}) copy-start(bf16[512,2048]{1,0:T(8,128)(2,1)} %reshape.41) | copy-start | bytes 6291460
  102.7 76.8 %copy-start.2 = (f32[64,6]{0,1:T(8,128)S(1)}, f32[64,6]{0,1:T(8,128)}, u32[]{:S(2)}) copy-start(f32[64,6]{0,1:T(8,128)} %param.9) | copy-start | bytes 4612
  167.5 29.5 %all-to-all-start.1 = ((bf16[128,4,512]{2,1,0:T(4,128)(2,1)}), bf16[128,4,512]{2,1,0:T(4,128)(2,1)S(1)}, u32[]{:S(2)}, u32[]{:S(2)}) async-start(bf16[128,4,512]{2,1,0:T(4,128)(2,1)} %reshape.42), calls=%async_computation.2 | async-start | bytes 1048576 | tf_op jit(solution)/shard_map/all_to_all | solution.py:37
Sparse Core Ops, SparseCore 0:
  102.9 62.6 reduce-scatter.1
where the time goes:
time: 208 us; the launch traced here: 207 us
  waiting for transfers between devices  80.2 us (39%)
  blocking collectives  79.1 us (38%)
  between operations  13.5 us (6%)
  starting transfers between devices  11.8 us (6%)
  local copies, waits for them, and re-layouts  10.4 us (5%)
  matrix products  9.8 us (5%)
  other arithmetic  2.42 us (1%)
    reduce_scatter x1, waiting for transfers between devices, per_device(): lax.psum_scatter(partial_value.astype(jnp.bfloat16), 'tp', scatter_dimens...  62.8 us
    all_to_all x1, blocking collectives, per_device(): lax.all_to_all(outgoing, 'req', split_axis=0, concat_axis=0, tiled=True)  62.5 us
    all_to_all x1, waiting for transfers between devices, per_device(): lax.all_to_all(shares, 'req', split_axis=0, concat_axis=0, tiled=True)  17.4 us
    all_gather x1, blocking collectives, per_device(): whole_rows = lax.all_gather(tokens, 'tp', axis=1, tiled=True)  16.6 us
    all_to_all x1, starting transfers between devices, per_device(): lax.all_to_all(shares, 'req', split_axis=0, concat_axis=0, tiled=True)  11.8 us
    dot_general x1, matrix products, per_device(): jnp.dot(hidden, expert_down[0], preferred_element_type=jnp.float32)  5.09 us
  transfers between devices with their start and end apart: 2, of which 2 were waited for; matrix products, arithmetic and copies ran while one was open for 0% of the time, Pallas kernels for 0%

commit v1 on v0

v1 whole, which is shorter than its diff:
```python
import jax
import jax.numpy as jnp
from jax import lax
from jax.experimental import pallas as pl
from jax.experimental.pallas import tpu as pltpu
from jax.sharding import PartitionSpec as P

MESH = pl.DeviceIdType.MESH
TOK, TOP, CAP = 64, 6, 4
PLANE, RUN, RING = 32, 4, 8
ROWS = PLANE * RUN * CAP
GRP, FFG = 512, 352
HALF = 2 * GRP
MBLK = 256


def kernel(tok, rt, wt, win_hbm, wdn_hbm, out,
           win, wdn, tok_all, meta, xsend, xrecv, xoth, psend, precv, pown, sbuf, back,
           cw_hi, cw_lo, rsend, rrecv,
           w_sem, tok_s, tok_r, meta_s, meta_r, x_s, x_r, o_s, o_r, p_s, p_r, b_s, b_r,
           q_s, q_r):
    req, tp = lax.axis_index("req"), lax.axis_index("tp")
    zlo, here = lax.div(req, PLANE), lax.rem(req, PLANE)
    zhi, core = lax.div(tp, 2), lax.rem(tp, 2)
    z = zhi * RUN + zlo

    def in_plane(d):
        other = lax.rem(here + d, PLANE)
        return other, (zlo * PLANE + other, tp)

    def in_ring(d):
        other = lax.rem(z + d, RING)
        return other, (lax.rem(other, RUN) * PLANE + here, lax.div(other, RUN) * 2 + core)

    mate = (req, zhi * 2 + 1 - core)

    def remote(src, dst, s, r, to):
        return pltpu.make_async_remote_copy(
            src_ref=src, dst_ref=dst, send_sem=s, recv_sem=r, device_id=to, device_id_type=MESH)

    w_in = pltpu.make_async_copy(win_hbm, win, w_sem.at[0])
    w_dn = pltpu.make_async_copy(wdn_hbm, wdn, w_sem.at[1])
    w_in.start()
    w_dn.start()

    barrier = pltpu.get_barrier_semaphore()

    @pl.loop(1, RING)
    def _(d):
        pl.semaphore_signal(barrier, inc=1, device_id=in_ring(d)[1], device_id_type=MESH)

    pl.semaphore_signal(barrier, inc=1, device_id=mate, device_id_type=MESH)

    @pl.loop(1, PLANE)
    def _(d):
        pl.semaphore_signal(barrier, inc=1, device_id=in_plane(d)[1], device_id_type=MESH)

    routes = rt[...]
    erow = lax.broadcasted_iota(jnp.int32, (128, 128), 0)
    lane = lax.broadcasted_iota(jnp.int32, (128, 128), 1)
    named = erow == routes[0:1, :]
    for k in range(1, TOP):
        named = named | (erow == routes[k:k + 1, :])
    earlier = (erow < lax.rem(lane, TOK)).astype(jnp.bfloat16)
    count = jnp.dot(named.astype(jnp.bfloat16), earlier, preferred_element_type=jnp.float32)
    meta[zlo, 8:16, :] = wt[...]
    meta[zlo, 0:8, :] = jnp.full((8, 128), -16.0, jnp.float32)
    for k in range(TOP):
        chosen = routes[k:k + 1, :]
        slot = jnp.sum(jnp.where(erow == chosen, count, 0.0), axis=0, keepdims=True)
        meta[zlo, k:k + 1, :] = chosen.astype(jnp.float32) * 16.0 + slot
    tok_all[z] = tok[...]

    pl.semaphore_wait(barrier, RING - 1 + 1 + PLANE - 1)

    def run_copy(d):
        other = lax.rem(zlo + d, RUN)
        return other, remote(meta.at[zlo], meta.at[zlo], meta_s.at[d], meta_r.at[zlo],
                             (other * PLANE + here, tp))

    @pl.loop(1, RUN)
    def _(d):
        run_copy(d)[1].start()

    @pl.loop(1, RING)
    def _(d):
        remote(tok, tok_all.at[z], tok_s.at[d], tok_r.at[z], in_ring(d)[1]).start()

    @pl.loop(1, RUN)
    def _(d):
        other, copy = run_copy(d)
        remote(meta.at[other], meta.at[other], meta_s.at[d], meta_r.at[other],
               (other * PLANE + here, tp)).wait_recv()
        copy.wait_send()

    low = lax.broadcasted_iota(jnp.int32, (8, 128), 1) < TOK
    base = -16.0 * PLANE * zlo.astype(jnp.float32)
    row = lax.broadcasted_iota(jnp.int32, (ROWS, 128), 0).astype(jnp.float32)
    picks = []
    for pair in range(2):
        a, b = 2 * pair, 2 * pair + 1
        keys = jnp.where(low, meta[a, 0:8, :] + 4.0 * a, meta[b, 0:8, :] + 4.0 * b) + base
        weights = jnp.where(low, meta[a, 8:16, :], meta[b, 8:16, :])
        pick = jnp.zeros((ROWS, 128), jnp.float32)
        scaled = jnp.zeros((ROWS, 128), jnp.float32)
        for k in range(TOP):
            hit = row == keys[k:k + 1, :]
            pick = jnp.where(hit, 1.0, pick)
            scaled = jnp.where(hit, weights[k:k + 1, :], scaled)
        picks.append(pick.astype(jnp.bfloat16))
        hi = scaled.astype(jnp.bfloat16)
        cw_hi[:, pair * 128:(pair + 1) * 128] = hi
        cw_lo[:, pair * 128:(pair + 1) * 128] = (scaled - hi.astype(jnp.float32)).astype(jnp.bfloat16)
    pick = jnp.concatenate(picks, axis=1)

    @pl.loop(1, RING)
    def _(d):
        other, to = in_ring(d)
        remote(tok_all.at[other], tok_all.at[other], tok_s.at[d], tok_r.at[other], to).wait_recv()

    for half in range(2):
        rows = tok_all[half * RUN:(half + 1) * RUN].reshape(RUN * TOK, GRP)
        x = jnp.dot(pick, rows, preferred_element_type=jnp.float32).astype(jnp.bfloat16)
        xsend[:, :, half * GRP:(half + 1) * GRP] = x.reshape(PLANE, RUN * CAP, GRP)

    @pl.loop(1, PLANE)
    def _(d):
        other, to = in_plane(d)
        remote(xsend.at[other], xrecv.at[here], x_s.at[d], x_r.at[here], to).start()

    xrecv[here] = xsend[here]
    remote(xsend.at[here], xoth.at[here], o_s.at[here], o_r.at[here], mate).start()

    @pl.loop(1, PLANE)
    def _(d):
        other, to = in_plane(PLANE - d)
        remote(xrecv.at[other], xrecv.at[other], x_s.at[d], x_r.at[other], to).wait_recv()
        remote(xrecv.at[other], xoth.at[other], o_s.at[other], o_r.at[other], mate).start()

    @pl.loop(0, PLANE)
    def _(i):
        remote(xoth.at[i], xoth.at[i], o_s.at[i], o_r.at[i], mate).wait_recv()

    w_in.wait()
    w_dn.wait()

    nsrc = MBLK // (RUN * CAP)

    def times_in(x, which, group):
        col = pl.ds(pl.multiple_of(group * GRP, GRP), GRP)
        return lax.dot_general(x, win[which, :, col], (((1,), (1,)), ((), ())),
                               preferred_element_type=jnp.float32)

    def part_copy(m):
        at = pl.ds(pl.multiple_of(m * MBLK, MBLK), MBLK)
        return remote(psend.at[at], precv.at[at], p_s.at[m], p_r.at[m], mate)

    @pl.loop(0, ROWS // MBLK)
    def _(m):
        src = pl.ds(m * nsrc, nsrc)
        at = pl.ds(pl.multiple_of(m * MBLK, MBLK), MBLK)
        own = xrecv[src].reshape(MBLK, HALF)
        oth = xoth[src].reshape(MBLK, HALF)
        sums = []
        for which in range(2):
            total = times_in(own[:, :GRP], which, core) + times_in(own[:, GRP:], which, 2 + core)
            total += times_in(oth[:, :GRP], which, 1 - core) + times_in(oth[:, GRP:], which, 3 - core)
            sums.append(total)
        gate, up = sums
        hidden = (gate / (1.0 + jnp.exp(-gate)) * up).astype(jnp.bfloat16)
        for half in range(2):
            col = pl.ds(pl.multiple_of((half * 2 + 1 - core) * GRP, GRP), GRP)
            part = jnp.dot(hidden, wdn[:, col], preferred_element_type=jnp.float32)
            psend[at, half * GRP:(half + 1) * GRP] = part.astype(jnp.bfloat16)
        part_copy(m).start()
        for half in range(2):
            col = pl.ds(pl.multiple_of((half * 2 + core) * GRP, GRP), GRP)
            pown[at, half * GRP:(half + 1) * GRP] = jnp.dot(
                hidden, wdn[:, col], preferred_element_type=jnp.float32)

    @pl.loop(0, ROWS // MBLK)
    def _(m):
        at = pl.ds(pl.multiple_of(m * MBLK, MBLK), MBLK)
        part_copy(m).wait()
        total = pown[at, :] + precv[at, :].astype(jnp.float32)
        sbuf[pl.ds(m * nsrc, nsrc)] = total.astype(jnp.bfloat16).reshape(nsrc, RUN * CAP, HALF)

    @pl.loop(1, PLANE)
    def _(d):
        other, to = in_plane(d)
        remote(sbuf.at[other], back.at[here], b_s.at[d], b_r.at[here], to).start()

    back[here] = sbuf[here]

    @pl.loop(1, PLANE)
    def _(d):
        other, to = in_plane(PLANE - d)
        remote(back.at[other], back.at[other], b_s.at[d], b_r.at[other], to).wait_recv()

    contract = (((0,), (0,)), ((), ()))
    for half in range(2):
        rows = back[:, :, half * GRP:(half + 1) * GRP].reshape(ROWS, GRP)
        mixed = lax.dot_general(cw_hi[...], rows, contract, preferred_element_type=jnp.float32)
        mixed += lax.dot_general(cw_lo[...], rows, contract, preferred_element_type=jnp.float32)
        rsend[half * RUN:(half + 1) * RUN] = mixed.astype(jnp.bfloat16).reshape(RUN, TOK, GRP)

    @pl.loop(1, RING)
    def _(d):
        other, to = in_ring(d)
        remote(rsend.at[other], rrecv.at[z], q_s.at[d], q_r.at[z], to).start()

    rrecv[z] = rsend[z]

    @pl.loop(1, RING)
    def _(d):
        other, to = in_ring(d)
        remote(rrecv.at[other], rrecv.at[other], q_s.at[d], q_r.at[other], to).wait_recv()

    total = rrecv[0].astype(jnp.float32)
    for i in range(1, RING):
        total += rrecv[i].astype(jnp.float32)
    out[...] = total.astype(jnp.bfloat16)

    @pl.loop(1, RING)
    def _(d):
        other, to = in_ring(d)
        remote(tok, tok_all.at[z], tok_s.at[d], tok_r.at[z], to).wait_send()
        remote(rsend.at[other], rrecv.at[z], q_s.at[d], q_r.at[z], to).wait_send()

    @pl.loop(1, PLANE)
    def _(d):
        other, to = in_plane(d)
        remote(xsend.at[other], xrecv.at[here], x_s.at[d], x_r.at[here], to).wait_send()
        remote(sbuf.at[other], back.at[here], b_s.at[d], b_r.at[here], to).wait_send()

    @pl.loop(0, PLANE)
    def _(i):
        remote(xrecv.at[i], xoth.at[i], o_s.at[i], o_r.at[i], mate).wait_send()


def per_device(tokens, expert_in, expert_down, routes, route_weight):
    rt = jnp.pad(jnp.tile(routes.T, (1, 2)), ((0, 2), (0, 0)), constant_values=-1)
    wt = jnp.pad(jnp.tile(route_weight.T, (1, 2)), ((0, 2), (0, 0)))
    vmem = pl.BlockSpec(memory_space=pltpu.VMEM)
    hbm = pl.BlockSpec(memory_space=pl.ANY)
    bf16, f32 = jnp.bfloat16, jnp.float32
    chunk = (PLANE, RUN * CAP, HALF)
    dma = pltpu.SemaphoreType.DMA
    scratch = [
        pltpu.VMEM((2, FFG, 4 * GRP), bf16),
        pltpu.VMEM((FFG, 4 * GRP), bf16),
        pltpu.VMEM((RING, TOK, GRP), bf16),
        pltpu.VMEM((RUN, 16, 128), f32),
        pltpu.VMEM(chunk, bf16),
        pltpu.VMEM(chunk, bf16),
        pltpu.VMEM(chunk, bf16),
        pltpu.VMEM((ROWS, HALF), bf16),
        pltpu.VMEM((ROWS, HALF), bf16),
        pltpu.VMEM((ROWS, HALF), f32),
        pltpu.VMEM(chunk, bf16),
        pltpu.VMEM(chunk, bf16),
        pltpu.VMEM((ROWS, RUN * TOK), bf16),
        pltpu.VMEM((ROWS, RUN * TOK), bf16),
        pltpu.VMEM((RING, TOK, GRP), bf16),
        pltpu.VMEM((RING, TOK, GRP), bf16),
        dma((2,)),
        dma((RING,)), dma((RING,)), dma((RUN,)), dma((RUN,)),
        dma((PLANE,)), dma((PLANE,)), dma((PLANE,)), dma((PLANE,)),
        dma((ROWS // MBLK,)), dma((ROWS // MBLK,)),
        dma((PLANE,)), dma((PLANE,)),
        dma((RING,)), dma((RING,)),
    ]
    return pl.pallas_call(
        kernel,
        out_shape=jax.ShapeDtypeStruct((TOK, GRP), bf16),
        in_specs=[vmem, vmem, vmem, hbm, hbm],
        out_specs=vmem,
        scratch_shapes=scratch,
        compiler_params=pltpu.CompilerParams(
            collective_id=0, has_side_effects=True, vmem_limit_bytes=60 * 1024 * 1024),
        name="routed_experts",
    )(tokens, rt, wt, jnp.swapaxes(expert_in[0], 1, 2), expert_down.reshape(FFG, 4 * GRP))


def solution(mesh):
    placed = (
        P("req", "tp"),
        P("req", None, None, "tp"),
        P("req", "tp", None),
        P("req", None),
        P("req", None),
    )
    return jax.shard_map(
        per_device, mesh=mesh, in_specs=placed, out_specs=P("req", "tp"), check_vma=False
    )
```

time: 208 us -> 109 us (0.52)
  Pallas kernels: 0 us -> 104 us
  waiting for transfers between devices: 80.2 us -> 0 us
  blocking collectives: 79.1 us -> 0 us
  between operations: 13.5 us -> 0.01 us
  starting transfers between devices: 11.8 us -> 0 us
  matrix products: 9.8 us -> 0 us
  local copies, waits for them, and re-layouts: 10.4 us -> 4.21 us
  other arithmetic: 2.42 us -> 0 us
    pallas_call x0 -> x1, Pallas kernels: none -> 104 us  [per_device(): pl.pallas_call(kernel, out_shape=jax.ShapeDtypeStruct((TOK, GRP), bf16),...]
    reduce_scatter x1 -> x0, waiting for transfers between devices: 62.8 us -> none  [per_device(): lax.psum_scatter(partial_value.astype(jnp.bfloat16), 'tp', scatter_dimens...]
    all_to_all x1 -> x0, blocking collectives: 62.5 us -> none  [per_device(): lax.all_to_all(outgoing, 'req', split_axis=0, concat_axis=0, tiled=True)]
    all_to_all x1 -> x0, waiting for transfers between devices: 17.4 us -> none  [per_device(): lax.all_to_all(shares, 'req', split_axis=0, concat_axis=0, tiled=True)]
    all_gather x1 -> x0, blocking collectives: 16.6 us -> none  [per_device(): whole_rows = lax.all_gather(tokens, 'tp', axis=1, tiled=True)]
    all_to_all x1 -> x0, starting transfers between devices: 11.8 us -> none  [per_device(): lax.all_to_all(shares, 'req', split_axis=0, concat_axis=0, tiled=True)]
    dot_general x3 -> x0, matrix products: 9.8 us -> none  [the longest x1 5.09 us: per_device(): jnp.dot(hidden, expert_down[0], preferred_element_type=jnp.float32)]
    reshape x4 -> x0, local copies, waits for them, and re-layouts: 6.38 us -> none  [the longest x1 2.23 us: per_device(): outgoing = outgoing.reshape(experts_all, capacity, -1)]
  transfers between devices with their start and end apart: 2 -> 0, of which waited for: 2 -> 0; matrix products, arithmetic and copies ran while one was open for 0% -> 0% of each run, Pallas kernels for 0% -> 0%
where the time goes in v1:
time: 109 us; the launch traced here: 108 us
  Pallas kernels  104 us (95%)
  local copies, waits for them, and re-layouts  4.21 us (4%)
    pallas_call x1, Pallas kernels, per_device(): pl.pallas_call(kernel, out_shape=jax.ShapeDtypeStruct((TOK, GRP), bf16),...  104 us

profile of v1, /device:TPU:1, one launch (start us, length us, event | category | flops | bytes accessed | tf_op | source)
XLA Modules:
  0.0 107.9 jit_solution(4929966801864481460)
XLA Ops:
  0.0 0.7 tile.8
  0.7 0.1 tile.9
  0.8 0.6 pad.8.rt
  1.4 0.7 tile.20
  2.1 0.1 tile.21
  2.1 0.6 pad.9.wt
  2.7 103.7 %routed_experts.1 = bf16[64,512]{1,0:T(8,128)(2,1)} custom-call(bf16[64,512]{1,0:T(8,128)(2,1)} %tok.1, s32[8,128]{1,0:T(8,128)} %pad.8.rt, f32[8,128]{1,0:T(8,128)} %pad.9.wt, bf16[2,352,2048]{2,1,0:T(8,128)(2,1)} %bitcast.6, bf16[352,2048]{1,0:T(8,128)(2,1)} %bitcast.7), custom_call_target="tpu_custom_call" | custom-call | tf_op jit(solution)/shard_map/routed_experts/pallas_call | solution.py:273
  106.4 1.5 %copy.7 = bf16[64,512]{1,0:T(8,128)(2,1)} copy(bf16[64,512]{1,0:T(8,128)(2,1)} %routed_experts.1) | data formatting | bytes 131072

commit v2 on v1

v2 whole, which is shorter than its diff:
```python
import jax
import jax.numpy as jnp
from jax import lax
from jax.experimental import pallas as pl
from jax.experimental.pallas import tpu as pltpu
from jax.sharding import PartitionSpec as P

MESH = pl.DeviceIdType.MESH
TOK, TOP, CAP = 64, 6, 4
PLANE, RUN, RING = 32, 4, 8
ROWS = PLANE * RUN * CAP
GRP, FFG = 512, 352
NEAR, FAR = 0, 1
STEPS = 4
MBLK = ROWS // STEPS


def kernel(tok, rt, wt, win_hbm, wdn_hbm, out,
           win, wdn, tok_all, meta, xsend, xrecv, xoth, psend, precv, pown, sbuf, back,
           cw_hi, cw_lo, rsend, rrecv,
           w_sem, tok_s, tok_r, meta_s, meta_r, x_s, x_r, o_s, o_r, p_s, p_r, b_s, b_r,
           q_s, q_r):
    req, tp = lax.axis_index("req"), lax.axis_index("tp")
    zlo, here = lax.div(req, PLANE), lax.rem(req, PLANE)
    y, x = lax.div(here, 4), lax.rem(here, 4)
    zhi, core = lax.div(tp, 2), lax.rem(tp, 2)
    z = zhi * RUN + zlo
    side = (zhi, 1 - zhi)

    def in_plane(other):
        return (zlo * PLANE + other, tp)

    def in_ring(other):
        return (lax.rem(other, RUN) * PLANE + here, lax.div(other, RUN) * 2 + core)

    def near_z(d):
        return zhi * RUN + lax.rem(zlo + d, RUN)

    def far_z(d):
        return (1 - zhi) * RUN + lax.rem(zlo + d, RUN)

    mate = (req, zhi * 2 + 1 - core)

    def remote(src, dst, s, r, to):
        return pltpu.make_async_remote_copy(
            src_ref=src, dst_ref=dst, send_sem=s, recv_sem=r, device_id=to, device_id_type=MESH)

    w_in = pltpu.make_async_copy(win_hbm, win, w_sem.at[0])
    w_dn = pltpu.make_async_copy(wdn_hbm, wdn, w_sem.at[1])
    w_in.start()
    w_dn.start()

    barrier = pltpu.get_barrier_semaphore()

    @pl.loop(1, RING)
    def _(d):
        pl.semaphore_signal(barrier, inc=1, device_id=in_ring(lax.rem(z + d, RING)),
                            device_id_type=MESH)

    pl.semaphore_signal(barrier, inc=1, device_id=mate, device_id_type=MESH)

    @pl.loop(1, PLANE)
    def _(d):
        pl.semaphore_signal(barrier, inc=1, device_id=in_plane(lax.rem(here + d, PLANE)),
                            device_id_type=MESH)

    routes = jnp.concatenate([rt[...], rt[...]], axis=1)
    erow = lax.broadcasted_iota(jnp.int32, (128, 128), 0)
    lane = lax.broadcasted_iota(jnp.int32, (128, 128), 1)
    named = erow == routes[0:1, :]
    for k in range(1, TOP):
        named = named | (erow == routes[k:k + 1, :])
    earlier = (erow < lax.rem(lane, TOK)).astype(jnp.bfloat16)
    count = jnp.dot(named.astype(jnp.bfloat16), earlier, preferred_element_type=jnp.float32)
    meta[zlo] = jnp.full((16, 128), -16.0, jnp.float32)
    meta[zlo, 8:8 + TOP, :] = jnp.concatenate([wt[...], wt[...]], axis=1)
    for k in range(TOP):
        chosen = routes[k:k + 1, :]
        slot = jnp.sum(jnp.where(erow == chosen, count, 0.0), axis=0, keepdims=True)
        meta[zlo, k:k + 1, :] = chosen.astype(jnp.float32) * 16.0 + slot
    tok_all[z] = tok[...]

    pl.semaphore_wait(barrier, RING - 1 + 1 + PLANE - 1)

    def meta_to(d):
        return remote(meta.at[zlo], meta.at[zlo], meta_s.at[d], meta_r.at[zlo],
                      in_ring(near_z(d)))

    def tok_to(other):
        return remote(tok, tok_all.at[z], tok_s.at[other], tok_r.at[z], in_ring(other))

    def tok_from(other):
        return remote(tok, tok_all.at[other], tok_s.at[other], tok_r.at[other], in_ring(other))

    @pl.loop(1, RUN)
    def _(d):
        meta_to(d).start()

    @pl.loop(1, RUN)
    def _(d):
        tok_to(near_z(d)).start()

    @pl.loop(1, RUN)
    def _(d):
        other = lax.rem(zlo + d, RUN)
        remote(meta.at[other], meta.at[other], meta_s.at[d], meta_r.at[other],
               in_ring(near_z(d))).wait_recv()

    low = lax.broadcasted_iota(jnp.int32, (8, 128), 1) < TOK
    base = -16.0 * PLANE * zlo.astype(jnp.float32)
    row = lax.broadcasted_iota(jnp.int32, (ROWS, 128), 0).astype(jnp.float32)

    def keys_of(pair):
        a, b = 2 * pair, 2 * pair + 1
        return jnp.where(low, meta[a, 0:8, :] + 4.0 * a, meta[b, 0:8, :] + 4.0 * b) + base

    picks = []
    for pair in range(2):
        keys = keys_of(pair)
        hit = row == keys[0:1, :]
        for k in range(1, TOP):
            hit = hit | (row == keys[k:k + 1, :])
        picks.append(hit.astype(jnp.bfloat16))
    pick = jnp.concatenate(picks, axis=1)

    def fill(half):
        rows = tok_all[pl.ds(side[half] * RUN, RUN)].reshape(RUN * TOK, GRP)
        got = jnp.dot(pick, rows, preferred_element_type=jnp.float32).astype(jnp.bfloat16)
        xsend[half] = got.reshape(PLANE, RUN * CAP, GRP)

    def block(m, which):
        off = lax.rem(8 - m, 8) if which == 0 else m + 1
        return off

    def send_rows(half):
        @pl.loop(1, PLANE)
        def _(i):
            m, r = lax.div(i, 8), lax.rem(i, 8)
            off = jnp.where(r < 4, lax.rem(8 - m, 8), m + 1)
            other = lax.rem(y + 8 - off, 8) * 4 + lax.rem(x + r, 4)
            remote(xsend.at[half, other], xrecv.at[half, here], x_s.at[half, other],
                   x_r.at[half, here], in_plane(other)).start()
        xrecv[half, here] = xsend[half, here]

    @pl.loop(1, RUN)
    def _(d):
        tok_from(near_z(d)).wait_recv()

    @pl.loop(0, RUN)
    def _(d):
        tok_to(far_z(d)).start()

    fill(NEAR)
    send_rows(NEAR)

    for pair in range(2):
        keys = keys_of(pair)
        weights = jnp.where(low, meta[2 * pair, 8:16, :], meta[2 * pair + 1, 8:16, :])
        scaled = jnp.zeros((ROWS, 128), jnp.float32)
        for k in range(TOP):
            scaled = jnp.where(row == keys[k:k + 1, :], weights[k:k + 1, :], scaled)
        hi = scaled.astype(jnp.bfloat16)
        cw_hi[:, pair * 128:(pair + 1) * 128] = hi
        cw_lo[:, pair * 128:(pair + 1) * 128] = (scaled - hi.astype(jnp.float32)).astype(jnp.bfloat16)

    @pl.loop(0, RUN)
    def _(d):
        tok_from(far_z(d)).wait_recv()

    fill(FAR)
    send_rows(FAR)

    def pass_on(half, line):
        at = pl.ds(line * 4, 4)
        return remote(xrecv.at[half, at], xoth.at[half, at], o_s.at[half, line],
                      o_r.at[half, line], mate)

    def arrive(half, off):
        line = lax.rem(y + off, 8)

        @pl.loop(0, 4)
        def _(i):
            other = line * 4 + i

            @pl.when(other != here)
            def _():
                remote(xrecv.at[half, other], xrecv.at[half, other], x_s.at[half, other],
                       x_r.at[half, other], in_plane(other)).wait_recv()
        pass_on(half, line).start()

    @pl.loop(0, STEPS)
    def _(m):
        for which in range(2):
            arrive(NEAR, block(m, which))

    w_in.wait()
    w_dn.wait()

    def times_in(lhs, which, group):
        col = pl.ds(pl.multiple_of(group * GRP, GRP), GRP)
        return lax.dot_general(lhs, win[which, :, col], (((1,), (1,)), ((), ())),
                               preferred_element_type=jnp.float32)

    def times_down(hidden, group):
        col = pl.ds(pl.multiple_of(group * GRP, GRP), GRP)
        return jnp.dot(hidden, wdn[:, col], preferred_element_type=jnp.float32)

    def part_copy(m):
        return remote(psend.at[m], precv.at[m], p_s.at[m], p_r.at[m], mate)

    def lines_of(m):
        return [lax.rem(y + block(m, which), 8) for which in range(2)]

    def send_back(half, line):
        @pl.loop(0, 4)
        def _(i):
            other = line * 4 + lax.rem(x + i, 4)

            @pl.when(other != here)
            def _():
                remote(sbuf.at[half, other], back.at[half, here], b_s.at[half, other],
                       b_r.at[half, here], in_plane(other)).start()

    def finish(m):
        part_copy(m).wait_recv()
        for half in (FAR, NEAR):
            total = pown[m, half] + precv[m, half].astype(jnp.float32)
            total = total.astype(jnp.bfloat16).reshape(2, 4, RUN * CAP, GRP)
            for which, line in enumerate(lines_of(m)):
                sbuf[half, pl.ds(line * 4, 4)] = total[which]
        for line in lines_of(m):
            send_back(FAR, line)

    @pl.loop(0, STEPS)
    def _(m):
        for which in range(2):
            arrive(FAR, block(m, which))

        @pl.when(m > 0)
        def _():
            finish(m - 1)

        lines = lines_of(m)
        for line in lines:
            for half in range(2):
                pass_on(half, line).wait_recv()
        parts = []
        for buf, of in ((xrecv, core), (xoth, 1 - core)):
            for half in range(2):
                lhs = jnp.concatenate(
                    [buf[half, pl.ds(line * 4, 4)].reshape(MBLK // 2, GRP) for line in lines], axis=0)
                parts.append((lhs, side[half] * 2 + of))
        gate = sum(times_in(lhs, 0, group) for lhs, group in parts)
        up = sum(times_in(lhs, 1, group) for lhs, group in parts)
        hidden = (gate / (1.0 + jnp.exp(-gate)) * up).astype(jnp.bfloat16)
        for half in range(2):
            psend[m, half] = times_down(hidden, side[half] * 2 + 1 - core).astype(jnp.bfloat16)
        part_copy(m).start()
        for half in range(2):
            pown[m, half] = times_down(hidden, side[half] * 2 + core)

    finish(STEPS - 1)

    @pl.loop(0, STEPS)
    def _(m):
        for line in lines_of(m):
            send_back(NEAR, line)

    contract = (((0,), (0,)), ((), ()))

    def ring_copy(dest):
        return remote(rsend.at[dest], rrecv.at[z], q_s.at[dest], q_r.at[z], in_ring(dest))

    def mix(half):
        back[half, here] = sbuf[half, here]

        @pl.loop(1, PLANE)
        def _(d):
            other = lax.rem(here + d, PLANE)
            remote(back.at[half, other], back.at[half, other], b_s.at[half, other],
                   b_r.at[half, other], in_plane(other)).wait_recv()
        rows = back[half].reshape(ROWS, GRP)
        mixed = lax.dot_general(cw_hi[...], rows, contract, preferred_element_type=jnp.float32)
        mixed += lax.dot_general(cw_lo[...], rows, contract, preferred_element_type=jnp.float32)
        rsend[pl.ds(side[half] * RUN, RUN)] = mixed.astype(jnp.bfloat16).reshape(RUN, TOK, GRP)

    mix(FAR)

    @pl.loop(0, RUN)
    def _(d):
        ring_copy(far_z(d)).start()

    mix(NEAR)

    @pl.loop(1, RUN)
    def _(d):
        ring_copy(near_z(d)).start()

    rrecv[z] = rsend[z]

    @pl.loop(1, PLANE)
    def _(d):
        other = lax.rem(here + d, PLANE)
        for half in range(2):
            remote(xsend.at[half, other], xrecv.at[half, here], x_s.at[half, other],
                   x_r.at[half, here], in_plane(other)).wait_send()
            remote(sbuf.at[half, other], back.at[half, here], b_s.at[half, other],
                   b_r.at[half, here], in_plane(other)).wait_send()

    @pl.loop(0, 8)
    def _(line):
        for half in range(2):
            pass_on(half, line).wait_send()

    @pl.loop(0, STEPS)
    def _(m):
        part_copy(m).wait_send()

    @pl.loop(1, RUN)
    def _(d):
        meta_to(d).wait_send()

    @pl.loop(1, RING)
    def _(d):
        tok_to(lax.rem(z + d, RING)).wait_send()

    @pl.loop(1, RING)
    def _(d):
        other = lax.rem(z + d, RING)
        remote(rrecv.at[other], rrecv.at[other], q_s.at[other], q_r.at[other],
               in_ring(other)).wait_recv()

    total = rrecv[0].astype(jnp.float32)
    for i in range(1, RING):
        total += rrecv[i].astype(jnp.float32)
    out[...] = total.astype(jnp.bfloat16)

    @pl.loop(1, RING)
    def _(d):
        ring_copy(lax.rem(z + d, RING)).wait_send()


def per_device(tokens, expert_in, expert_down, routes, route_weight):
    vmem = pl.BlockSpec(memory_space=pltpu.VMEM)
    hbm = pl.BlockSpec(memory_space=pl.ANY)
    bf16, f32 = jnp.bfloat16, jnp.float32
    chunks = (2, PLANE, RUN * CAP, GRP)
    part = (STEPS, 2, MBLK, GRP)
    dma = pltpu.SemaphoreType.DMA
    scratch = [
        pltpu.VMEM((2, FFG, 4 * GRP), bf16),
        pltpu.VMEM((FFG, 4 * GRP), bf16),
        pltpu.VMEM((RING, TOK, GRP), bf16),
        pltpu.VMEM((RUN, 16, 128), f32),
        pltpu.VMEM(chunks, bf16),
        pltpu.VMEM(chunks, bf16),
        pltpu.VMEM(chunks, bf16),
        pltpu.VMEM(part, bf16),
        pltpu.VMEM(part, bf16),
        pltpu.VMEM(part, f32),
        pltpu.VMEM(chunks, bf16),
        pltpu.VMEM(chunks, bf16),
        pltpu.VMEM((ROWS, RUN * TOK), bf16),
        pltpu.VMEM((ROWS, RUN * TOK), bf16),
        pltpu.VMEM((RING, TOK, GRP), bf16),
        pltpu.VMEM((RING, TOK, GRP), bf16),
        dma((2,)),
        dma((RING,)), dma((RING,)), dma((RUN,)), dma((RUN,)),
        dma((2, PLANE)), dma((2, PLANE)), dma((2, 8)), dma((2, 8)),
        dma((STEPS,)), dma((STEPS,)),
        dma((2, PLANE)), dma((2, PLANE)),
        dma((RING,)), dma((RING,)),
    ]
    return pl.pallas_call(
        kernel,
        out_shape=jax.ShapeDtypeStruct((TOK, GRP), bf16),
        in_specs=[vmem, vmem, vmem, hbm, hbm],
        out_specs=vmem,
        scratch_shapes=scratch,
        compiler_params=pltpu.CompilerParams(
            collective_id=0, has_side_effects=True, vmem_limit_bytes=60 * 1024 * 1024),
        name="routed_experts",
    )(tokens, routes.T, route_weight.T, jnp.swapaxes(expert_in[0], 1, 2),
      expert_down.reshape(FFG, 4 * GRP))


def solution(mesh):
    placed = (
        P("req", "tp"),
        P("req", None, None, "tp"),
        P("req", "tp", None),
        P("req", None),
        P("req", None),
    )
    return jax.shard_map(
        per_device, mesh=mesh, in_specs=placed, out_specs=P("req", "tp"), check_vma=False
    )
```

time: 109 us -> 93.5 us (0.86)
  the two profiles are of different devices: /device:TPU:1 before, /device:TPU:8 now
where the time goes in v2:
time: 93.5 us; the launch traced here: 93.3 us
  Pallas kernels  91.8 us (98%)
  local copies, waits for them, and re-layouts  1.47 us (2%)
    pallas_call x1, Pallas kernels, per_device(): pl.pallas_call(kernel, out_shape=jax.ShapeDtypeStruct((TOK, GRP), bf16),...  91.8 us

profile of v2, /device:TPU:8, one launch (start us, length us, event | category | flops | bytes accessed | tf_op | source)
XLA Modules:
  0.0 93.3 jit_solution(6953339902660105244)
XLA Ops:
  0.0 91.8 %routed_experts.1 = bf16[64,512]{1,0:T(8,128)(2,1)} custom-call(bf16[64,512]{1,0:T(8,128)(2,1)} %tok.1, s32[6,64]{1,0:T(8,128)} %bitcast.8, f32[6,64]{1,0:T(8,128)} %bitcast.9, bf16[2,352,2048]{2,1,0:T(8,128)(2,1)} %bitcast.6, bf16[352,2048]{1,0:T(8,128)(2,1)} %bitcast.7), custom_call_target="tpu_custom_call" | custom-call | tf_op jit(solution)/shard_map/routed_experts/pallas_call | solution.py:374
  91.8 1.5 %copy.7 = bf16[64,512]{1,0:T(8,128)(2,1)} copy(bf16[64,512]{1,0:T(8,128)(2,1)} %routed_experts.1) | data formatting | bytes 131072

commit v3 on v2

--- a/solution.py
+++ b/solution.py
@@ -11,7 +11,9 @@
 ROWS = PLANE * RUN * CAP
 GRP, FFG = 512, 352
 NEAR, FAR = 0, 1
-STEPS = 4
+LINES = ((3, 5), (4, 0), (6, 2), (7, 1))
+CROSS = (3, 5, 4)
+STEPS = len(LINES)
 MBLK = ROWS // STEPS
 
 
@@ -19,7 +21,7 @@
            win, wdn, tok_all, meta, xsend, xrecv, xoth, psend, precv, pown, sbuf, back,
            cw_hi, cw_lo, rsend, rrecv,
            w_sem, tok_s, tok_r, meta_s, meta_r, x_s, x_r, o_s, o_r, p_s, p_r, b_s, b_r,
-           q_s, q_r):
+           q_s, q_r, zsend, zrecv, zx_s, zx_r, zb_s, zb_r):
     req, tp = lax.axis_index("req"), lax.axis_index("tp")
     zlo, here = lax.div(req, PLANE), lax.rem(req, PLANE)
     y, x = lax.div(here, 4), lax.rem(here, 4)
@@ -40,6 +42,7 @@
         return (1 - zhi) * RUN + lax.rem(zlo + d, RUN)
 
     mate = (req, zhi * 2 + 1 - core)
+    opposite = (req, (1 - zhi) * 2 + core)
 
     def remote(src, dst, s, r, to):
         return pltpu.make_async_remote_copy(
@@ -128,18 +131,22 @@
         got = jnp.dot(pick, rows, preferred_element_type=jnp.float32).astype(jnp.bfloat16)
         xsend[half] = got.reshape(PLANE, RUN * CAP, GRP)
 
-    def block(m, which):
-        off = lax.rem(8 - m, 8) if which == 0 else m + 1
-        return off
+    def line_at(off):
+        return lax.rem(y + off, 8)
+
+    def crossing(half, off):
+        return half == FAR and off in CROSS
 
     def send_rows(half):
-        @pl.loop(1, PLANE)
-        def _(i):
-            m, r = lax.div(i, 8), lax.rem(i, 8)
-            off = jnp.where(r < 4, lax.rem(8 - m, 8), m + 1)
-            other = lax.rem(y + 8 - off, 8) * 4 + lax.rem(x + r, 4)
-            remote(xsend.at[half, other], xrecv.at[half, here], x_s.at[half, other],
-                   x_r.at[half, here], in_plane(other)).start()
+        for off in sum(LINES, ()):
+            if crossing(half, off):
+                continue
+
+            @pl.loop(1 if off == 0 else 0, 4)
+            def _(i):
+                other = line_at(8 - off) * 4 + lax.rem(x + i, 4)
+                remote(xsend.at[half, other], xrecv.at[half, here], x_s.at[half, other],
+                       x_r.at[half, here], in_plane(other)).start()
         xrecv[half, here] = xsend[half, here]
 
     @pl.loop(1, RUN)
@@ -175,23 +182,30 @@
         return remote(xrecv.at[half, at], xoth.at[half, at], o_s.at[half, line],
                       o_r.at[half, line], mate)
 
+    def cross_rows(off):
+        line = line_at(off)
+        at = pl.ds(line * 4, 4)
+        return remote(xrecv.at[NEAR, at], xrecv.at[FAR, at], zx_s.at[line], zx_r.at[line], opposite)
+
     def arrive(half, off):
-        line = lax.rem(y + off, 8)
-
-        @pl.loop(0, 4)
-        def _(i):
-            other = line * 4 + i
-
-            @pl.when(other != here)
-            def _():
-                remote(xrecv.at[half, other], xrecv.at[half, other], x_s.at[half, other],
-                       x_r.at[half, other], in_plane(other)).wait_recv()
+        line = line_at(off)
+        if crossing(half, off):
+            cross_rows(off).wait_recv()
+        else:
+            @pl.loop(0, 4)
+            def _(i):
+                other = line * 4 + i
+
+                @pl.when(other != here)
+                def _():
+                    remote(xrecv.at[half, other], xrecv.at[half, other], x_s.at[half, other],
+                           x_r.at[half, other], in_plane(other)).wait_recv()
+            if off in CROSS:
+                cross_rows(off).start()
         pass_on(half, line).start()
 
-    @pl.loop(0, STEPS)
-    def _(m):
-        for which in range(2):
-            arrive(NEAR, block(m, which))
+    for off in sum(LINES, ()):
+        arrive(NEAR, off)
 
     w_in.wait()
     w_dn.wait()
@@ -208,39 +222,54 @@
     def part_copy(m):
         return remote(psend.at[m], precv.at[m], p_s.at[m], p_r.at[m], mate)
 
-    def lines_of(m):
-        return [lax.rem(y + block(m, which), 8) for which in range(2)]
-
-    def send_back(half, line):
-        @pl.loop(0, 4)
+    def send_back(half, off):
+        @pl.loop(1 if off == 0 else 0, 4)
         def _(i):
-            other = line * 4 + lax.rem(x + i, 4)
-
-            @pl.when(other != here)
-            def _():
-                remote(sbuf.at[half, other], back.at[half, here], b_s.at[half, other],
-                       b_r.at[half, here], in_plane(other)).start()
+            other = line_at(off) * 4 + lax.rem(x + i, 4)
+            remote(sbuf.at[half, other], back.at[half, here], b_s.at[half, other],
+                   b_r.at[half, here], in_plane(other)).start()
+
+    def cross_back(off):
+        k = CROSS.index(off)
+        return remote(zsend.at[k], zrecv.at[k], zb_s.at[k], zb_r.at[k], opposite)
 
     def finish(m):
         part_copy(m).wait_recv()
         for half in (FAR, NEAR):
             total = pown[m, half] + precv[m, half].astype(jnp.float32)
             total = total.astype(jnp.bfloat16).reshape(2, 4, RUN * CAP, GRP)
-            for which, line in enumerate(lines_of(m)):
-                sbuf[half, pl.ds(line * 4, 4)] = total[which]
-        for line in lines_of(m):
-            send_back(FAR, line)
-
-    @pl.loop(0, STEPS)
-    def _(m):
-        for which in range(2):
-            arrive(FAR, block(m, which))
-
-        @pl.when(m > 0)
-        def _():
+            for which, off in enumerate(LINES[m]):
+                if crossing(half, off):
+                    zsend[CROSS.index(off)] = total[which]
+                else:
+                    sbuf[half, pl.ds(line_at(off) * 4, 4)] = total[which]
+            if half == FAR:
+                for off in LINES[m]:
+                    if off in CROSS:
+                        cross_back(off).start()
+                    else:
+                        send_back(FAR, off)
+
+    def settle(m):
+        for off in LINES[m]:
+            if off in CROSS:
+                cross_back(off).wait_recv()
+                at = pl.ds(line_at(off) * 4, 4)
+                total = sbuf[NEAR, at].astype(jnp.float32) + zrecv[CROSS.index(off)].astype(jnp.float32)
+                sbuf[NEAR, at] = total.astype(jnp.bfloat16)
+                send_back(NEAR, off)
+
+    for off in CROSS:
+        back[FAR, pl.ds(line_at(off) * 4, 4)] = jnp.zeros((4, RUN * CAP, GRP), jnp.bfloat16)
+
+    for m in range(STEPS):
+        for off in LINES[m]:
+            arrive(FAR, off)
+        if m >= 1:
             finish(m - 1)
-
-        lines = lines_of(m)
+        if m >= 2:
+            settle(m - 2)
+        lines = [line_at(off) for off in LINES[m]]
         for line in lines:
             for half in range(2):
                 pass_on(half, line).wait_recv()
@@ -260,11 +289,11 @@
             pown[m, half] = times_down(hidden, side[half] * 2 + core)
 
     finish(STEPS - 1)
-
-    @pl.loop(0, STEPS)
-    def _(m):
-        for line in lines_of(m):
-            send_back(NEAR, line)
+    for m in range(STEPS - 2, STEPS):
+        settle(m)
+    for off in sum(LINES, ()):
+        if off not in CROSS:
+            send_back(NEAR, off)
 
     contract = (((0,), (0,)), ((), ()))
 
@@ -274,11 +303,15 @@
     def mix(half):
         back[half, here] = sbuf[half, here]
 
-        @pl.loop(1, PLANE)
-        def _(d):
-            other = lax.rem(here + d, PLANE)
-            remote(back.at[half, other], back.at[half, other], b_s.at[half, other],
-                   b_r.at[half, other], in_plane(other)).wait_recv()
+        for off in sum(LINES, ()):
+            if crossing(half, off):
+                continue
+
+            @pl.loop(1 if off == 0 else 0, 4)
+            def _(i):
+                other = line_at(off) * 4 + lax.rem(x + i, 4)
+                remote(back.at[half, other], back.at[half, other], b_s.at[half, other],
+                       b_r.at[half, other], in_plane(other)).wait_recv()
         rows = back[half].reshape(ROWS, GRP)
         mixed = lax.dot_general(cw_hi[...], rows, contract, preferred_element_type=jnp.float32)
         mixed += lax.dot_general(cw_lo[...], rows, contract, preferred_element_type=jnp.float32)
@@ -298,14 +331,20 @@
 
     rrecv[z] = rsend[z]
 
-    @pl.loop(1, PLANE)
-    def _(d):
-        other = lax.rem(here + d, PLANE)
+    for off in sum(LINES, ()):
         for half in range(2):
-            remote(xsend.at[half, other], xrecv.at[half, here], x_s.at[half, other],
-                   x_r.at[half, here], in_plane(other)).wait_send()
-            remote(sbuf.at[half, other], back.at[half, here], b_s.at[half, other],
-                   b_r.at[half, here], in_plane(other)).wait_send()
+            if crossing(half, off):
+                cross_rows(off).wait_send()
+                cross_back(off).wait_send()
+                continue
+
+            @pl.loop(1 if off == 0 else 0, 4)
+            def _(i):
+                other = line_at(off) * 4 + lax.rem(x + i, 4)
+                remote(xsend.at[half, other], xrecv.at[half, here], x_s.at[half, other],
+                       x_r.at[half, here], in_plane(other)).wait_send()
+                remote(sbuf.at[half, other], back.at[half, here], b_s.at[half, other],
+                       b_r.at[half, here], in_plane(other)).wait_send()
 
     @pl.loop(0, 8)
     def _(line):
@@ -370,6 +409,9 @@
         dma((STEPS,)), dma((STEPS,)),
         dma((2, PLANE)), dma((2, PLANE)),
         dma((RING,)), dma((RING,)),
+        pltpu.VMEM((len(CROSS), 4, RUN * CAP, GRP), bf16),
+        pltpu.VMEM((len(CROSS), 4, RUN * CAP, GRP), bf16),
+        dma((8,)), dma((8,)), dma((len(CROSS),)), dma((len(CROSS),)),
     ]
     return pl.pallas_call(
         kernel,

time: 93.5 us -> 101 us (1.080)
  the two profiles are of different devices: /device:TPU:8 before, /device:TPU:63 now
where the time goes in v3:
time: 101 us
  Pallas kernels  99 us (98%)
  local copies, waits for them, and re-layouts  1.47 us (1%)
    pallas_call x1, Pallas kernels, per_device(): pl.pallas_call(kernel, out_shape=jax.ShapeDtypeStruct((TOK, GRP), bf16),...  99 us

profile of v3, /device:TPU:63, one launch (start us, length us, event | category | flops | bytes accessed | tf_op | source)
XLA Modules:
  0.0 100.5 jit_solution(16632591961547634227)
XLA Ops:
  0.0 99.0 %routed_experts.1 = bf16[64,512]{1,0:T(8,128)(2,1)} custom-call(bf16[64,512]{1,0:T(8,128)(2,1)} %tok.1, s32[6,64]{1,0:T(8,128)} %bitcast.8, f32[6,64]{1,0:T(8,128)} %bitcast.9, bf16[2,352,2048]{2,1,0:T(8,128)(2,1)} %bitcast.6, bf16[352,2048]{1,0:T(8,128)(2,1)} %bitcast.7), custom_call_target="tpu_custom_call" | custom-call | tf_op jit(solution)/shard_map/routed_experts/pallas_call | solution.py:416
  99.1 1.5 %copy.7 = bf16[64,512]{1,0:T(8,128)(2,1)} copy(bf16[64,512]{1,0:T(8,128)(2,1)} %routed_experts.1) | data formatting | bytes 131072

commit v4 on v3

--- a/solution.py
+++ b/solution.py
@@ -11,8 +11,8 @@
 ROWS = PLANE * RUN * CAP
 GRP, FFG = 512, 352
 NEAR, FAR = 0, 1
-LINES = ((3, 5), (4, 0), (6, 2), (7, 1))
-CROSS = (3, 5, 4)
+LINES = ((4, 0), (3, 5), (6, 2), (7, 1))
+CROSS = (4,)
 STEPS = len(LINES)
 MBLK = ROWS // STEPS
 

time: 101 us -> 86.9 us (0.86)
  the two profiles are of different devices: /device:TPU:63 before, /device:TPU:1 now
where the time goes in v4:
time: 86.9 us; the launch traced here: 86.6 us
  Pallas kernels  85.1 us (98%)
  local copies, waits for them, and re-layouts  1.47 us (2%)
    pallas_call x1, Pallas kernels, per_device(): pl.pallas_call(kernel, out_shape=jax.ShapeDtypeStruct((TOK, GRP), bf16),...  85.1 us

profile of v4, /device:TPU:1, one launch (start us, length us, event | category | flops | bytes accessed | tf_op | source)
XLA Modules:
  0.0 86.6 jit_solution(12632739018191160842)
XLA Ops:
  0.0 85.1 %routed_experts.1 = bf16[64,512]{1,0:T(8,128)(2,1)} custom-call(bf16[64,512]{1,0:T(8,128)(2,1)} %tok.1, s32[6,64]{1,0:T(8,128)} %bitcast.8, f32[6,64]{1,0:T(8,128)} %bitcast.9, bf16[2,352,2048]{2,1,0:T(8,128)(2,1)} %bitcast.6, bf16[352,2048]{1,0:T(8,128)(2,1)} %bitcast.7), custom_call_target="tpu_custom_call" | custom-call | tf_op jit(solution)/shard_map/routed_experts/pallas_call | solution.py:416
  85.1 1.5 %copy.7 = bf16[64,512]{1,0:T(8,128)(2,1)} copy(bf16[64,512]{1,0:T(8,128)(2,1)} %routed_experts.1) | data formatting | bytes 131072

commit v5 on v4

--- a/solution.py
+++ b/solution.py
@@ -149,13 +149,13 @@
                        x_r.at[half, here], in_plane(other)).start()
         xrecv[half, here] = xsend[half, here]
 
+    @pl.loop(0, RUN)
+    def _(d):
+        tok_to(far_z(d)).start()
+
     @pl.loop(1, RUN)
     def _(d):
         tok_from(near_z(d)).wait_recv()
-
-    @pl.loop(0, RUN)
-    def _(d):
-        tok_to(far_z(d)).start()
 
     fill(NEAR)
     send_rows(NEAR)
@@ -166,9 +166,10 @@
         scaled = jnp.zeros((ROWS, 128), jnp.float32)
         for k in range(TOP):
             scaled = jnp.where(row == keys[k:k + 1, :], weights[k:k + 1, :], scaled)
+        scaled = scaled.T
         hi = scaled.astype(jnp.bfloat16)
-        cw_hi[:, pair * 128:(pair + 1) * 128] = hi
-        cw_lo[:, pair * 128:(pair + 1) * 128] = (scaled - hi.astype(jnp.float32)).astype(jnp.bfloat16)
+        cw_hi[pair * 128:(pair + 1) * 128, :] = hi
+        cw_lo[pair * 128:(pair + 1) * 128, :] = (scaled - hi.astype(jnp.float32)).astype(jnp.bfloat16)
 
     @pl.loop(0, RUN)
     def _(d):
@@ -295,7 +296,6 @@
         if off not in CROSS:
             send_back(NEAR, off)
 
-    contract = (((0,), (0,)), ((), ()))
 
     def ring_copy(dest):
         return remote(rsend.at[dest], rrecv.at[z], q_s.at[dest], q_r.at[z], in_ring(dest))
@@ -313,8 +313,8 @@
                 remote(back.at[half, other], back.at[half, other], b_s.at[half, other],
                        b_r.at[half, other], in_plane(other)).wait_recv()
         rows = back[half].reshape(ROWS, GRP)
-        mixed = lax.dot_general(cw_hi[...], rows, contract, preferred_element_type=jnp.float32)
-        mixed += lax.dot_general(cw_lo[...], rows, contract, preferred_element_type=jnp.float32)
+        mixed = jnp.dot(cw_hi[...], rows, preferred_element_type=jnp.float32)
+        mixed += jnp.dot(cw_lo[...], rows, preferred_element_type=jnp.float32)
         rsend[pl.ds(side[half] * RUN, RUN)] = mixed.astype(jnp.bfloat16).reshape(RUN, TOK, GRP)
 
     mix(FAR)
@@ -399,8 +399,8 @@
         pltpu.VMEM(part, f32),
         pltpu.VMEM(chunks, bf16),
         pltpu.VMEM(chunks, bf16),
-        pltpu.VMEM((ROWS, RUN * TOK), bf16),
-        pltpu.VMEM((ROWS, RUN * TOK), bf16),
+        pltpu.VMEM((RUN * TOK, ROWS), bf16),
+        pltpu.VMEM((RUN * TOK, ROWS), bf16),
         pltpu.VMEM((RING, TOK, GRP), bf16),
         pltpu.VMEM((RING, TOK, GRP), bf16),
         dma((2,)),

time: 86.9 us -> 86.7 us (level)
  no operation moved by 1% of the time
where the time goes in v5:
time: 86.7 us; the launch traced here: 86.5 us
  Pallas kernels  85 us (98%)
  local copies, waits for them, and re-layouts  1.47 us (2%)
    pallas_call x1, Pallas kernels, per_device(): pl.pallas_call(kernel, out_shape=jax.ShapeDtypeStruct((TOK, GRP), bf16),...  85 us

profile of v5, /device:TPU:1, one launch (start us, length us, event | category | flops | bytes accessed | tf_op | source)
XLA Modules:
  0.0 86.5 jit_solution(9000842338115021931)
XLA Ops:
  0.0 85.0 %routed_experts.1 = bf16[64,512]{1,0:T(8,128)(2,1)} custom-call(bf16[64,512]{1,0:T(8,128)(2,1)} %tok.1, s32[6,64]{1,0:T(8,128)} %bitcast.8, f32[6,64]{1,0:T(8,128)} %bitcast.9, bf16[2,352,2048]{2,1,0:T(8,128)(2,1)} %bitcast.6, bf16[352,2048]{1,0:T(8,128)(2,1)} %bitcast.7), custom_call_target="tpu_custom_call" | custom-call | tf_op jit(solution)/shard_map/routed_experts/pallas_call | solution.py:416
  85.0 1.5 %copy.7 = bf16[64,512]{1,0:T(8,128)(2,1)} copy(bf16[64,512]{1,0:T(8,128)(2,1)} %routed_experts.1) | data formatting | bytes 131072
